TPU v7x, 128 devices: a whole 4x4x4 slice. The times are simulated.
128 devices in a mesh: section: 4 (over z), dp: 32 (over y, x, core).
Axes of the slice: x: 4, y: 4, z: 4, core: 2. Of those that a mesh axis runs over, the one named last changes fastest.
Arguments:
- hidden: bfloat16 [64, 4, 8192], P('dp')
- delta: float32 [64, 8192], P('dp'), may hold values from -12 to 12
- gain: float32 [8192], replicated, may hold values from 0.5 to 1.5
- head: bfloat16 [131072, 8192], P(('section', 'dp'))
- targets: int32 [64, 3], replicated, may hold values from 0 to 131071
- tlen: int32 [64], replicated, may hold values from 1 to 3, as said below
Outputs:
- edit_loss: float32 [64], P('dp')
- value_step: float32 [64, 8192], P('dp')
Inputs may be any that keep to these rules, and one draw needn't show every extreme that they name: Entries of targets at positions tlen or later are not read.
All inputs are finite; a program needn't handle non-finite values.
Results may differ from a plain program's by a relative error of at most 0.0003.
The roundings to bfloat16 on the way count: a program that leaves them out, or rounds other values in their place, can miss the bound.
Values may be sent and summed in bfloat16 or wider, within the bound.
A program may use at most 128 MiB of HBM per device.

v0:
```python
import jax
import jax.numpy as jnp
from jax import lax
from jax.sharding import PartitionSpec as P

TGT = 3
EPS = 1e-05
KL_WEIGHT = 0.0625
STEP_RATE = 10.0


def normalize(values, gain):
    inv = lax.rsqrt(jnp.mean(values * values, axis=-1, keepdims=True) + EPS)
    return (values * inv * gain, inv)


def local(hidden, delta, gain, head, targets, tlen):
    edit_dev, slots, width = hidden.shape
    voc_dev = head.shape[0]
    edits = targets.shape[0]
    every = ("section", "dp")
    hid = hidden.astype(jnp.float32)
    shifted = hid + delta[:, None, :]
    normed, inv = normalize(shifted, gain)
    base, unused = normalize(hid[:, slots - 1, :], gain)
    rows = jnp.concatenate(
        [normed.astype(jnp.bfloat16), base.astype(jnp.bfloat16)[:, None, :]], axis=1
    )
    logits = lax.dot_general(
        lax.all_gather(rows, "dp", axis=0, tiled=True),
        head,
        (((2,), (1,)), ((), ())),
        preferred_element_type=jnp.float32,
    )
    local_top = jnp.max(logits, axis=-1)
    local_exp = jnp.exp(logits - local_top[:, :, None])
    local_total = jnp.sum(local_exp, axis=-1)
    gap = jnp.sum(local_exp[:, TGT + 1, :] * (logits[:, TGT + 1, :] - logits[:, TGT, :]), axis=-1)
    vocab_ids = lax.axis_index(every) * voc_dev + jnp.arange(voc_dev, dtype=jnp.int32)
    hit = targets[:, :, None] == vocab_ids[None, None, :]
    tgt_local = jnp.sum(jnp.where(hit, logits[:, :TGT, :], 0.0), axis=-1)
    packed = jnp.concatenate(
        [
            local_top.reshape(-1),
            local_total.reshape(-1),
            gap,
            tgt_local.reshape(-1),
            inv.reshape(-1),
        ]
    )
    every_stat = lax.all_gather(packed, every)
    n = edits * (TGT + 2)
    tops = every_stat[:, :n].reshape(-1, edits, TGT + 2)
    top = jnp.max(tops, axis=0)
    factor = jnp.exp(tops - top[None])
    total = jnp.sum(every_stat[:, n : 2 * n].reshape(-1, edits, TGT + 2) * factor, axis=0)
    gap_all = jnp.sum(every_stat[:, 2 * n : 2 * n + edits] * factor[:, :, TGT + 1], axis=0)
    first = 2 * n + edits
    tgt_sum = jnp.sum(every_stat[:, first : first + edits * TGT], axis=0).reshape(edits, TGT)
    dp = lax.axis_size("dp")
    inv_all = every_stat[:dp, first + edits * TGT :].reshape(edits, slots)
    logz = top + jnp.log(total)
    kl = gap_all / total[:, TGT + 1] - logz[:, TGT + 1] + logz[:, TGT]
    logp = logits - logz[:, :, None]
    tgt_logp = tgt_sum - logz[:, :TGT]
    lengths = tlen.astype(jnp.float32)
    weight = (jnp.arange(TGT, dtype=jnp.int32)[None, :] < tlen[:, None]).astype(
        jnp.float32
    ) / lengths[:, None]
    nll = -jnp.sum(tgt_logp * weight, axis=1)
    loss_all = nll + KL_WEIGHT * kl
    offset = lax.axis_index("dp") * edit_dev
    edit_loss = lax.dynamic_slice_in_dim(loss_all, offset, edit_dev, 0)
    probs = jnp.exp(logp)
    d_target = (probs[:, :TGT, :] - hit.astype(jnp.float32)) * weight[:, :, None]
    d_kl = KL_WEIGHT * (probs[:, TGT, :] - probs[:, TGT + 1, :])
    dlogits = jnp.concatenate([d_target, d_kl[:, None, :]], axis=1).astype(jnp.bfloat16)
    inner_local = jnp.sum(dlogits.astype(jnp.float32) * logits[:, :slots, :], axis=-1)
    gnorm = jnp.einsum("esv,vd->sed", dlogits, head, preferred_element_type=jnp.float32)
    mixed = jnp.sum(gnorm * inv_all.T[:, :, None], axis=0)
    full, inner = lax.psum((mixed, inner_local), every)
    mine = lax.dynamic_slice_in_dim(full, offset, edit_dev, 0)
    mine_inner = lax.dynamic_slice_in_dim(inner, offset, edit_dev, 0)[:, :, None]
    back = jnp.sum(shifted * (inv * inv * mine_inner / width), axis=1)
    value_step = -STEP_RATE * (gain * mine - back)
    return (edit_loss, value_step)


def solution(mesh):
    placed = (P("dp", None, None), P("dp", None), P(), P(("section", "dp"), None), P(), P())
    return jax.shard_map(
        local, mesh=mesh, in_specs=placed, out_specs=(P("dp"), P("dp", None)), check_vma=False
    )
```

profile of v0, /device:TPU:1, one launch (start us, length us, event | category | flops | bytes accessed | tf_op | source)
XLA Modules:
  0.0 408.3 jit_solution(15002139512185290136)
XLA Ops:
  7.2 0.9 convert_element_type.27
  8.3 1.1 multiply_reduce_fusion.1
  9.6 0.9 multiply_convert_fusion.1
  10.5 1.1 multiply_convert_fusion
  11.6 0.8 pad_maximum_fusion.2
  12.6 56.3 %all-gather.3.cloned.1.call-done = bf16[64,5,8192]{2,1,0:T(8,128)(2,1)} async-done(((bf16[2,5,8192]{2,1,0:T(8,128)(2,1)}), bf16[64,5,8192]{2,1,0:T(8,128)(2,1)}) %all-gather.3.cloned.1.call-update) | async-done | bytes 5242896 | tf_op jit(solution)/shard_map/all_gather | solution.py:30
  68.9 15.8 %fusion.30 = (f32[64,5]{0,1:T(8,128)S(1)}, f32[64,5,1024]{2,0,1:T(8,128)S(1)}) fusion(bf16[1024,8192]{1,0:T(8,128)(2,1)} %param.9, bf16[64,5,8192]{2,1,0:T(8,128)(2,1)} %all-gather.3.cloned.1.call-done), kind=kOutput, calls=%fused_computation.55 | convolution fusion | flops 5369036288 | bytes 23332096 | tf_op jit(solution)/shard_map/dot_general | solution.py:29
  84.8 0.3 fusion.28
  86.2 0.3 dynamic-update-slice
  86.5 0.8 copy-done.1
  87.6 145.2 %all-reduce.6.cloned.1.call-done = f32[115712]{0:T(1024)} async-done(((f32[115712]{0:T(1024)}), f32[115712]{0:T(1024)}) %all-reduce.6.cloned.1.call-update) | async-done | bytes 462864
  232.8 1.5 reshape.134
  234.3 0.7 fusion.29
  235.6 0.3 copy-done.9
  236.7 0.7 convert_divide_fusion
  237.4 0.7 copy.42
  238.0 0.7 fusion.20
  238.7 0.9 fusion.18
  239.8 11.8 %fusion.11 = f32[64,8192]{1,0:T(8,128)} fusion(f32[4,64]{1,0:T(4,128)S(1)} %copy.43, bf16[1024,8192]{1,0:T(8,128)(2,1)} %param.9, bf16[64,1,1024]{2,0,1:T(8,128)(2,1)} %fusion.20, bf16[64,3,1024]{2,0,1:T(8,128)(2,1)S(1)} %fusion.18), kind=kOutput, calls=%fused_computation.7 | convolution fusion | flops 4298899456 | bytes 19399680 | tf_op jit(solution)/shard_map/esv,vd->sed/dot_general | solution.py:79
  251.7 0.7 copy-done.10
  252.7 63.7 %psum.15 = f32[64,4]{0,1:T(4,128)S(1)} all-reduce(f32[64,4]{0,1:T(4,128)S(1)} %fusion.14), channel_id=1, replica_groups=mesh['section'=4,'dp'=32] {'section','dp'}, use_global_device_ids=true, to_apply=%region_14.15 | all-reduce | flops 256 | bytes 2048 | tf_op jit(solution)/shard_map/psum | solution.py:81
  317.3 0.6 dynamic_slice.9
  318.1 82.0 %all-reduce.4.cloned.1.call-done = f32[64,8192]{1,0:T(8,128)} async-done(((f32[64,8192]{1,0:T(8,128)}), f32[64,8192]{1,0:T(8,128)}) %all-reduce.4.cloned.1.call-update) | async-done | bytes 2097168 | tf_op jit(solution)/shard_map/psum | solution.py:81
  400.1 1.6 subtract_multiply_fusion
  (81 shorter events, 4.9 us)
Async XLA Ops:
  7.2 61.7 %all-gather.3.cloned.1.call-start = ((), (), s32[]{:S(2)}) async-start(), calls=%async_computation | async-start | bytes 8650752 | tf_op jit(solution)/shard_map/all_gather | solution.py:30
  9.5 3.1 copy-start.13
  12.5 220.4 %all-reduce.6.cloned.1.call-start = ((), (), s32[]{:S(2)}) async-start(), calls=%async_computation.2 | async-start | bytes 925696
  12.6 72.9 %copy-start.12 = (s32[1024]{0:T(1024)}, s32[1024]{0:T(1024)S(1)}, u32[]{:S(2)}) copy-start(s32[1024]{0:T(1024)S(1)} %iota_add_fusion) | copy-start | bytes 12292
  84.7 0.8 copy-start.15
  84.8 2.8 copy-start.17
  86.5 0.8 copy-start.1
  87.3 312.8 %all-reduce.4.cloned.1.call-start = ((), (), s32[]{:S(2)}) async-start(), calls=%async_computation.1 | async-start | bytes 4194304 | tf_op jit(solution)/shard_map/psum | solution.py:81
  235.3 0.6 copy-start.9
  235.6 0.6 copy-start.7
  236.2 1.9 copy-start.2
  251.6 0.8 copy-start.10
  251.6 0.9 copy-start.6
  251.6 64.8 %copy-start.14 = (f32[2,4]{0,1:T(4,128)S(1)}, f32[2,4]{0,1:T(4,128)}, u32[]{:S(2)}) copy-start(f32[2,4]{0,1:T(4,128)} %copy-done.13) | copy-start | bytes 100
  251.6 65.1 %copy-start.4 = (f32[128,320]{1,0:T(8,128)S(1)}, f32[128,320]{1,0:T(8,128)}, u32[]{:S(2)}) copy-start(f32[128,320]{1,0:T(8,128)} %get-tuple-element.6) | copy-start | bytes 491524
  251.6 65.4 %copy-start.3 = (f32[64,5]{1,0:T(8,128)S(1)}, f32[64,5]{1,0:T(8,128)}, u32[]{:S(2)}) copy-start(f32[64,5]{1,0:T(8,128)} %copy-done.2) | copy-start | bytes 3844
  251.6 65.4 %copy-start.8 = (f32[64,5]{1,0:T(8,128)S(1)}, f32[64,5]{1,0:T(8,128)}, u32[]{:S(2)}) copy-start(f32[64,5]{1,0:T(8,128)} %copy-done.7) | copy-start | bytes 3844
  251.6 65.6 %copy-start.16 = (f32[64]{0:T(128)S(1)}, f32[64]{0:T(128)}, u32[]{:S(2)}) copy-start(f32[64]{0:T(128)} %get-tuple-element.9) | copy-start | bytes 772
  251.6 66.2 %copy-start = (bf16[2,4,8192]{2,1,0:T(4,128)(2,1)S(1)}, bf16[2,4,8192]{2,1,0:T(4,128)(2,1)}, u32[]{:S(2)}) copy-start(bf16[2,4,8192]{2,1,0:T(4,128)(2,1)} %param.6) | copy-start | bytes 393220
  251.6 66.2 %copy-start.5 = (f32[2,8192]{1,0:T(2,128)S(1)}, f32[2,8192]{1,0:T(2,128)}, u32[]{:S(2)}) copy-start(f32[2,8192]{1,0:T(2,128)} %param.7) | copy-start | bytes 196612
  251.7 148.5 %copy-start.11 = (f32[8192]{0:T(1024)S(1)}, f32[8192]{0:T(1024)}, u32[]{:S(2)}) copy-start(f32[8192]{0:T(1024)} %param.8) | copy-start | bytes 98308
Sparse Core Ops, SparseCore 0:
  12.6 56.2 all-gather.2
  87.5 145.3 all-reduce.5
  251.8 148.2 all-reduce.3
where the time goes:
time: 409 us; the launch traced here: 408 us
  waiting for transfers between devices  284 us (69%)
  blocking collectives  63.7 us (16%)
  matrix products  27.6 us (7%)
  between operations  14 us (3%)
  other arithmetic  11.4 us (3%)
  local copies, waits for them, and re-layouts  7.68 us (2%)
    unnamed x4, waiting for transfers between devices  145 us
    psum x1, waiting for transfers between devices, local(): full, inner = lax.psum((mixed, inner_local), every)  82 us
    psum x1, blocking collectives, local(): full, inner = lax.psum((mixed, inner_local), every)  63.7 us
    all_gather x1, waiting for transfers between devices, local(): lax.all_gather(rows, 'dp', axis=0, tiled=True)  56.3 us
    dot_general x1, matrix products, local(): lax.dot_general(lax.all_gather(rows, 'dp', axis=0, tiled=True), head, (((...  15.8 us
    dot_general x1, matrix products, local(): jnp.einsum('esv,vd->sed', dlogits, head, preferred_element_type=jnp.float32)  11.8 us
  transfers between devices with their start and end apart: 3, of which 3 were waited for; matrix products, arithmetic and copies ran while one was open for 0% of the time, Pallas kernels for 0%

commit v1 on v0

--- a/solution.py
+++ b/solution.py
@@ -26,11 +26,12 @@
     rows = jnp.concatenate(
         [normed.astype(jnp.bfloat16), base.astype(jnp.bfloat16)[:, None, :]], axis=1
     )
+    arrange_thing = lambda local_array: jnp.concatenate(
+        jax.lax.all_to_all(jnp.stack(jax.lax.axis_size("dp") * [local_array], axis=0), "dp", 0, 0),
+        axis=0,
+    )
     logits = lax.dot_general(
-        lax.all_gather(rows, "dp", axis=0, tiled=True),
-        head,
-        (((2,), (1,)), ((), ())),
-        preferred_element_type=jnp.float32,
+        arrange_thing(rows), head, (((2,), (1,)), ((), ())), preferred_element_type=jnp.float32
     )
     local_top = jnp.max(logits, axis=-1)
     local_exp = jnp.exp(logits - local_top[:, :, None])

time: 409 us -> 451 us (1.10)
  local copies, waits for them, and re-layouts: 7.68 us -> 38.9 us
  starting transfers between devices: 0.3 us -> 9.11 us
  waiting for transfers between devices: 284 us -> 290 us
  matrix products: 27.6 us -> 22.7 us
    all_to_all x0 -> x1, waiting for transfers between devices: none -> 61.6 us  [local(): jax.lax.all_to_all(jnp.stack(jax.lax.axis_size('dp') * [local_array], axi...]
    all_gather x1 -> x0, waiting for transfers between devices: 56.3 us -> none  [local(): lax.all_gather(rows, 'dp', axis=0, tiled=True)]
    all_to_all x0 -> x1, local copies, waits for them, and re-layouts: none -> 14.4 us  [local(): jax.lax.all_to_all(jnp.stack(jax.lax.axis_size('dp') * [local_array], axi...]
    reshape x0 -> x1, local copies, waits for them, and re-layouts: none -> 8.69 us  [local(): jnp.concatenate(jax.lax.all_to_all(jnp.stack(jax.lax.axis_size('dp') * [l...]
    all_to_all x0 -> x1, starting transfers between devices: none -> 8.62 us  [local(): jax.lax.all_to_all(jnp.stack(jax.lax.axis_size('dp') * [local_array], axi...]
    another operation x0 -> x1, local copies, waits for them, and re-layouts: none -> 7.61 us  [local(): jnp.stack(jax.lax.axis_size('dp') * [local_array], axis=0)]
    dot_general x1, matrix products: 15.8 us -> 10.8 us  [local(): lax.dot_general(arrange_thing(rows), head, (((2,), (1,)), ((), ())), pref...]
    unnamed x4 -> x3, waiting for transfers between devices: 145 us -> 147 us
where the time goes in v1:
time: 451 us; the launch traced here: 450 us
  waiting for transfers between devices  290 us (64%)
  blocking collectives  64.2 us (14%)
  local copies, waits for them, and re-layouts  38.9 us (9%)
  matrix products  22.7 us (5%)
  between operations  14.4 us (3%)
  other arithmetic  10.6 us (2%)
  starting transfers between devices  9.11 us (2%)
    unnamed x3, waiting for transfers between devices  147 us
    psum x1, waiting for transfers between devices, local(): full, inner = lax.psum((mixed, inner_local), every)  81.5 us
    psum x1, blocking collectives, local(): full, inner = lax.psum((mixed, inner_local), every)  64.2 us
    all_to_all x1, waiting for transfers between devices, local(): jax.lax.all_to_all(jnp.stack(jax.lax.axis_size('dp') * [local_array], axi...  61.6 us
    all_to_all x1, local copies, waits for them, and re-layouts, local(): jax.lax.all_to_all(jnp.stack(jax.lax.axis_size('dp') * [local_array], axi...  14.4 us
    dot_general x1, matrix products, local(): jnp.einsum('esv,vd->sed', dlogits, head, preferred_element_type=jnp.float32)  11.8 us
    dot_general x1, matrix products, local(): lax.dot_general(arrange_thing(rows), head, (((2,), (1,)), ((), ())), pref...  10.8 us
  transfers between devices with their start and end apart: 3, of which 3 were waited for; matrix products, arithmetic and copies ran while one was open for 0% of the time, Pallas kernels for 0%

profile of v1, /device:TPU:1, one launch (start us, length us, event | category | flops | bytes accessed | tf_op | source)
XLA Modules:
  0.0 450.2 jit_solution(5405288272446656469)
XLA Ops:
  7.2 0.9 convert_element_type.27
  8.3 1.1 multiply_reduce_fusion.1
  9.9 0.9 multiply_convert_fusion.1
  10.8 1.1 multiply_convert_fusion
  12.2 7.6 %stack.2 = bf16[32,2,5,8192]{3,1,2,0:T(2,128)(2,1)} broadcast(bf16[2,5,8192]{2,0,1:T(2,128)(2,1)S(1)} %copy.39), dimensions={1,2,3} | broadcast | bytes 5406720 | tf_op jit(solution)/shard_map/stack | solution.py:30
  19.8 8.6 %all-to-all-start = ((bf16[32,2,5,8192]{3,1,2,0:T(2,128)(2,1)}), bf16[32,2,5,8192]{3,1,2,0:T(2,128)(2,1)}, u32[]{:S(2)}, u32[]{:S(2)}) async-start(bf16[32,2,5,8192]{3,1,2,0:T(2,128)(2,1)} %stack.2), calls=%async_computation | async-start | bytes 10485760 | tf_op jit(solution)/shard_map/all_to_all | solution.py:30
  28.8 61.6 %all-to-all-done = bf16[32,2,5,8192]{3,1,2,0:T(2,128)(2,1)} async-done(((bf16[32,2,5,8192]{3,1,2,0:T(2,128)(2,1)}), bf16[32,2,5,8192]{3,1,2,0:T(2,128)(2,1)}, u32[]{:S(2)}, u32[]{:S(2)}) %all-to-all-start) | async-done | bytes 5242912 | tf_op jit(solution)/shard_map/all_to_all | solution.py:30
  90.3 14.4 %copy.40 = bf16[32,2,5,8192]{3,1,0,2:T(2,128)(2,1)} copy(bf16[32,2,5,8192]{3,1,2,0:T(2,128)(2,1)} %all-to-all-done) | data formatting | bytes 10485760 | tf_op jit(solution)/shard_map/all_to_all | solution.py:30
  104.7 8.7 %reshape.133 = bf16[64,5,8192]{2,0,1:T(8,128)(2,1)} reshape(bf16[32,2,5,8192]{3,1,0,2:T(2,128)(2,1)} %copy.40) | data formatting | bytes 10485760 | tf_op jit(solution)/shard_map/reshape | solution.py:29
  113.4 10.8 %fusion.29 = (f32[64,5]{0,1:T(8,128)S(1)}, f32[64,5,1024]{2,0,1:T(8,128)S(1)}) fusion(bf16[64,5,8192]{2,0,1:T(8,128)(2,1)} %reshape.133, bf16[1024,8192]{1,0:T(8,128)(2,1)} %param.9), kind=kOutput, calls=%fused_computation.54 | convolution fusion | flops 5369036288 | bytes 23332096 | tf_op jit(solution)/shard_map/dot_general | solution.py:33
  126.2 0.8 copy-done.1
  127.3 147.2 %all-reduce.6.cloned.1.call-done = f32[115712]{0:T(1024)} async-done(((f32[115712]{0:T(1024)}), f32[115712]{0:T(1024)}) %all-reduce.6.cloned.1.call-update) | async-done | bytes 462864
  274.5 1.5 reshape.140
  276.0 0.7 fusion.28
  278.3 0.7 convert_divide_fusion
  279.1 0.7 copy.48
  279.7 0.7 fusion.19
  280.4 0.9 fusion.17
  281.4 11.8 %fusion.10 = f32[64,8192]{1,0:T(8,128)} fusion(f32[4,64]{1,0:T(4,128)S(1)} %copy.49, bf16[1024,8192]{1,0:T(8,128)(2,1)} %param.9, bf16[64,1,1024]{2,0,1:T(8,128)(2,1)} %fusion.19, bf16[64,3,1024]{2,0,1:T(8,128)(2,1)S(1)} %fusion.17), kind=kOutput, calls=%fused_computation.6 | convolution fusion | flops 4298899456 | bytes 19399680 | tf_op jit(solution)/shard_map/esv,vd->sed/dot_general | solution.py:80
  293.4 0.7 copy-done.10
  295.2 0.6 dynamic_slice.9
  295.8 64.2 %psum.15 = f32[64,4]{1,0:T(8,128)S(1)} all-reduce(f32[64,4]{1,0:T(8,128)S(1)} %copy.50), channel_id=1, replica_groups=mesh['section'=4,'dp'=32] {'section','dp'}, use_global_device_ids=true, to_apply=%region_14.15 | all-reduce | flops 256 | bytes 2048 | tf_op jit(solution)/shard_map/psum | solution.py:82
  360.2 81.5 %all-reduce.4.cloned.1.call-done = f32[64,8192]{1,0:T(8,128)} async-done(((f32[64,8192]{1,0:T(8,128)}), f32[64,8192]{1,0:T(8,128)}) %all-reduce.4.cloned.1.call-update) | async-done | bytes 2097168 | tf_op jit(solution)/shard_map/psum | solution.py:82
  441.7 1.6 subtract_multiply_fusion
  (82 shorter events, 6.6 us)
Async XLA Ops:
  9.4 0.5 copy-start.13
  19.8 70.5 %all-to-all-start = ((bf16[32,2,5,8192]{3,1,2,0:T(2,128)(2,1)}), bf16[32,2,5,8192]{3,1,2,0:T(2,128)(2,1)}, u32[]{:S(2)}, u32[]{:S(2)}) async-start(bf16[32,2,5,8192]{3,1,2,0:T(2,128)(2,1)} %stack.2), calls=%async_computation | async-start | bytes 10485760 | tf_op jit(solution)/shard_map/all_to_all | solution.py:30
  28.4 246.1 %all-reduce.6.cloned.1.call-start = ((), (), s32[]{:S(2)}) async-start(), calls=%async_computation.2 | async-start | bytes 925696
  28.8 96.3 %copy-start.12 = (s32[1024]{0:T(1024)}, s32[1024]{0:T(1024)S(1)}, u32[]{:S(2)}) copy-start(s32[1024]{0:T(1024)S(1)} %iota_add_fusion) | copy-start | bytes 12292
  124.3 0.8 copy-start.15
  124.4 2.9 copy-start.17
  126.2 0.8 copy-start.1
  127.0 314.7 %all-reduce.4.cloned.1.call-start = ((), (), s32[]{:S(2)}) async-start(), calls=%async_computation.1 | async-start | bytes 4194304 | tf_op jit(solution)/shard_map/psum | solution.py:82
  277.0 0.6 copy-start.9
  277.2 0.6 copy-start.7
  277.9 1.9 copy-start.2
  293.3 0.8 copy-start.10
  293.3 0.9 copy-start.6
  293.3 1.3 copy-start.4
  293.3 1.6 copy-start.3
  293.3 1.6 copy-start.8
  293.3 1.9 copy-start.16
  293.3 66.6 %copy-start.14 = (f32[2,4]{1,0:T(2,128)S(1)}, f32[2,4]{1,0:T(2,128)}, u32[]{:S(2)}) copy-start(f32[2,4]{1,0:T(2,128)} %copy-done.13) | copy-start | bytes 100
  293.3 66.6 %copy-start = (bf16[2,4,8192]{2,1,0:T(4,128)(2,1)S(1)}, bf16[2,4,8192]{2,1,0:T(4,128)(2,1)}, u32[]{:S(2)}) copy-start(bf16[2,4,8192]{2,1,0:T(4,128)(2,1)} %param.6) | copy-start | bytes 393220
  293.3 66.6 %copy-start.5 = (f32[2,8192]{1,0:T(2,128)S(1)}, f32[2,8192]{1,0:T(2,128)}, u32[]{:S(2)}) copy-start(f32[2,8192]{1,0:T(2,128)} %param.7) | copy-start | bytes 196612
  293.4 148.3 %copy-start.11 = (f32[8192]{0:T(1024)S(1)}, f32[8192]{0:T(1024)}, u32[]{:S(2)}) copy-start(f32[8192]{0:T(1024)} %param.8) | copy-start | bytes 98308
Sparse Core Ops, SparseCore 0:
  127.1 147.3 all-reduce.5
  293.5 148.1 all-reduce.3
